TPU v7x, 32 devices: a whole 2x2x4 slice. The times are simulated.
32 devices in a mesh: group: 2 (over x), src: 16 (over z, y, core).
Axes of the slice: x: 2, y: 2, z: 4, core: 2. Of those that a mesh axis runs over, the one named last changes fastest.
Arguments:
- rcv_points: float32 [3, 4096], P(None, ('group', 'src')), parts along dimension 1, may hold values from -1 to 1
- rcv_normals: float32 [3, 4096], P(None, ('group', 'src')), parts along dimension 1, may hold values from -4 to 4
- left_modes: float32 [8, 4096], P(None, ('group', 'src')), parts along dimension 1, may hold values from -5 to 5
- vertices: float32 [3, 2048], P(None, ('group', 'src')), parts along dimension 1, may hold values from -1 to 1
- connect: int32 [2, 4096], P(None, ('group', 'src')), parts along dimension 1, may hold values from 0 to 1023, as said below
- right_modes: float32 [8, 4096], P(None, ('group', 'src')), parts along dimension 1, may hold values from -0.125 to 0.125
- mode_weights: float32 [16], P('group'), parts along dimension 0, may hold values from 0.25 to 1
Outputs:
- rcv_grad: float32 [6, 4096], P(None, ('group', 'src')), parts along dimension 1
- vert_grad: float32 [3, 2048], P(None, ('group', 'src')), parts along dimension 1
There are 2 independent parts, one for each index of `group`. A program takes and returns all parts, laid end to end along the dimension named above; each array names one. Nothing has to cross between parts.
Inputs may be any that keep to these rules, and one draw needn't show every extreme that they name: `connect`: a panel's first vertex is one of the 64 vertices held at the same index of src as the panel, and its second vertex is the next vertex number.
All inputs are finite; a program needn't handle non-finite values.
Results may differ from a plain program's by a relative error of at most 0.0003.
Values sent between devices are 32-bit elements; how exact they have to be, the bound alone decides.
No kernel may reach another device: no remote copies, remote signals or barrier semaphores. Data moves between devices by JAX's collectives and lax.ppermute only.
A program may use at most 64 MiB of HBM per device.

v0:
```python
import math
import jax
import jax.numpy as jnp
from jax import lax
from jax.sharding import PartitionSpec as P

core_term = 0.05
inverse_four_pi = 0.25 / math.pi


def shifted(value, axis, steps):
    count = lax.axis_size(axis)
    leading, last = (max(0, -steps), min(count, count - steps))
    return lax.ppermute(value, axis, [(source, source + steps) for source in range(leading, last)])


def lift_points(raw):
    return jnp.stack([raw[0], raw[1], 0.5 + 0.2 * raw[2]])


def place_points(raw):
    return jnp.stack([raw[0], raw[1], 0.2 * raw[2]])


def tile_energy(points, normals, first_end, second_end, coefficient):
    rel_first = points[:, None, :] - first_end[:, :, None]
    rel_second = points[:, None, :] - second_end[:, :, None]
    segment = (second_end - first_end)[:, :, None]
    cross_x = rel_first[1] * rel_second[2] - rel_first[2] * rel_second[1]
    cross_y = rel_first[2] * rel_second[0] - rel_first[0] * rel_second[2]
    cross_z = rel_first[0] * rel_second[1] - rel_first[1] * rel_second[0]
    cross_sq = cross_x * cross_x + cross_y * cross_y + cross_z * cross_z
    dist_first = jnp.sqrt(jnp.sum(rel_first * rel_first, axis=0))
    dist_second = jnp.sqrt(jnp.sum(rel_second * rel_second, axis=0))
    along_term = jnp.sum(segment * (rel_first / dist_first - rel_second / dist_second), axis=0)
    span_sq = jnp.sum(segment * segment, axis=0)
    denominator = cross_sq + core_term * (span_sq + 1.0)
    normal_term = (
        normals[0][None, :] * cross_x
        + normals[1][None, :] * cross_y
        + normals[2][None, :] * cross_z
    )
    influence = inverse_four_pi * normal_term * along_term / denominator
    return jnp.sum(coefficient * influence)


def tile_gradients(points, normals, first_end, second_end, coefficient):
    return jax.grad(tile_energy, argnums=(0, 1, 2, 3))(
        points, normals, first_end, second_end, coefficient
    )


def on_device(rcv_points, rcv_normals, left_modes, vertices, connect, right_modes, mode_weights):
    own_count = vertices.shape[1]
    next_first = shifted(vertices[:, :1], "src", -1)
    extended = jnp.concatenate([vertices, next_first], axis=1)
    places = place_points(extended)
    base_vertex = lax.axis_index("src") * own_count
    local_first = connect[0] - base_vertex
    local_second = local_first + 1
    first_end = places[:, local_first]
    second_end = places[:, local_second]
    points = lift_points(rcv_points)
    chain_scale = jnp.array([1.0, 1.0, 0.2], dtype=jnp.float32)[:, None]
    weighted = right_modes * mode_weights[:, None]
    receiver_count = rcv_points.shape[1] * lax.axis_size("src")
    source_count = connect.shape[1]
    start_totals = (
        jnp.zeros((3, source_count), jnp.float32),
        jnp.zeros((3, source_count), jnp.float32),
        jnp.zeros((6, receiver_count), jnp.float32),
    )
    shard_points = lax.all_gather(points, "src", axis=1, tiled=True)
    shard_normals = lax.all_gather(rcv_normals, "src", axis=1, tiled=True)
    shard_left = lax.all_gather(left_modes, "src", axis=1, tiled=True)
    row_count = shard_points.shape[1]
    width_rows = math.gcd(row_count, 2048)

    def advance(number, inner):
        sum_first, sum_second, receiver_buffer = inner
        local_start = number * width_rows
        block_points = lax.dynamic_slice_in_dim(shard_points, local_start, width_rows, 1)
        block_normals = lax.dynamic_slice_in_dim(shard_normals, local_start, width_rows, 1)
        block_left = lax.dynamic_slice_in_dim(shard_left, local_start, width_rows, 1)
        coefficient = jnp.einsum("mj,mi->ji", weighted, block_left, precision=lax.Precision.HIGHEST)
        grads = tile_gradients(block_points, block_normals, first_end, second_end, coefficient)
        rows_out = jnp.concatenate([grads[0] * chain_scale, grads[1]], axis=0)
        receiver_buffer = lax.dynamic_update_slice_in_dim(receiver_buffer, rows_out, local_start, 1)
        return (sum_first + grads[2], sum_second + grads[3], receiver_buffer)

    sum_first, sum_second, receiver_buffer = lax.fori_loop(
        0, row_count // width_rows, advance, start_totals
    )
    rcv_grad = lax.psum_scatter(receiver_buffer, "src", scatter_dimension=1, tiled=True)
    vertex_partial = jnp.zeros((3, own_count + 1), jnp.float32)
    vertex_partial = (
        vertex_partial.at[:, local_first].add(sum_first).at[:, local_second].add(sum_second)
    )
    incoming = shifted(vertex_partial[:, own_count:], "src", 1)
    own_part = vertex_partial[:, :own_count]
    own_part = jnp.concatenate([own_part[:, :1] + incoming, own_part[:, 1:]], axis=1)
    vert_grad = own_part * chain_scale
    return (rcv_grad, vert_grad)


def solution(mesh):
    in_specs = (
        P(None, ("group", "src")),
        P(None, ("group", "src")),
        P(None, ("group", "src")),
        P(None, ("group", "src")),
        P(None, ("group", "src")),
        P(None, ("group", "src")),
        P("group"),
    )
    out_specs = (P(None, ("group", "src")), P(None, ("group", "src")))
    return jax.shard_map(
        on_device, mesh=mesh, in_specs=in_specs, out_specs=out_specs, check_vma=False
    )
```

profile of v0, /device:TPU:0, one launch (start us, length us, event | category | flops | bytes accessed | tf_op | source)
XLA Modules:
  0.0 154.4 jit_solution(849035136935577808)
XLA Ops:
  7.2 0.0 reduce-scatter.2.cloned.1.call-start
  7.2 1.3 collective-permute-start
  8.5 0.7 multiply_add_fusion.1
  9.2 0.7 slice.81
  9.9 23.8 %all_gather.10 = f32[3,2048]{1,0:T(4,128)S(1)} all-gather(f32[3,128]{1,0:T(4,128)S(1)} %pad_maximum_fusion.3), channel_id=1, replica_groups=mesh['group'=2,'src'=16] {'src'}, dimensions={1}, use_global_device_ids=true | all-gather | bytes 26112 | tf_op jit(solution)/shard_map/all_gather | solution.py:73
  33.7 17.7 %all_gather.9 = f32[3,2048]{1,0:T(4,128)S(1)} all-gather(f32[3,128]{1,0:T(4,128)} %param.9), channel_id=1, replica_groups=mesh['group'=2,'src'=16] {'src'}, dimensions={1}, use_global_device_ids=true | all-gather | bytes 26112 | tf_op jit(solution)/shard_map/all_gather | solution.py:74
  51.4 19.2 %all_gather.11 = f32[8,2048]{1,0:T(8,128)S(1)} all-gather(f32[8,128]{1,0:T(8,128)} %param.10), channel_id=1, replica_groups=mesh['group'=2,'src'=16] {'src'}, dimensions={1}, use_global_device_ids=true | all-gather | bytes 69632 | tf_op jit(solution)/shard_map/all_gather | solution.py:75
  70.6 0.7 fusion.24
  71.3 0.0 collective-permute-done
  71.3 0.8 pad_maximum_fusion.1
  72.1 0.1 copy.26
  72.2 0.6 gather_fusion.1
  72.9 0.1 copy.29
  72.9 0.7 gather_fusion
  73.6 0.1 copy.27
  73.7 0.8 fusion.15
  74.5 0.0 copy-start.2
  74.5 0.0 copy-start.3
  74.6 0.3 multiply_divide_fusion.1
  74.9 0.3 multiply_divide_fusion.2
  75.3 0.0 copy-done.2
  75.3 0.0 copy-done.3
  75.3 1.8 %divide_multiply_fusion.1 = (f32[128,2048]{1,0:T(8,128)S(1)}, f32[128,2048]{1,0:T(8,128)S(1)}, f32[128,2048]{1,0:T(8,128)S(1)}, f32[128,2048]{1,0:T(8,128)S(1)},...) fusion(f32[128]{0:T(128)S(1)} %add_multiply_fusion.2, f32[2048]{0:T(1024)S(1)} %bitcast.136, ...), kind=kOutput, calls=%fused_computation.109 | convolution fusion | flops 31196160 | bytes 13726240 | tf_op jit(solution)/shard_map/while/body/eval_jaxpr/mj,mi->ji/dot_general | solution.py:85
  77.1 2.5 %multiply_reduce_fusion = (f32[3,128]{1,0:T(4,128)S(1)}, f32[128,2048]{1,0:T(8,128)S(1)}, f32[128,2048]{1,0:T(8,128)S(1)}, f32[128,2048]{1,0:T(8,128)S(1)}) fusion(f32[128,2048]{1,0:T(8,128)S(1)} %get-tuple-element.62, f32[128,2048]{1,0:T(8,128)S(1)} %get-tuple-element.92, f32[3,128]{1,0:T(4,128)S(1)} %bitcast.127, f32[128,2048]{1,0:T(8,128)S(1)} %get-tuple-element.94, ...), kind=kLoop, calls=%fused_computation.36 | loop fusion | flops 12582528 | bytes 8419328 | tf_op jit(solution)/shard_map/while/body/eval_jaxpr/transpose(jvp())/reduce_sum | solution.py:35
  79.6 0.2 multiply_multiply_fusion.3
  79.8 0.2 multiply_multiply_fusion.1
  80.1 0.6 fusion.28
  80.6 2.0 %multiply_bitcast_fusion.5 = (f32[1,128,2048]{2,1,0:T(8,128)}, f32[128,2048]{1,0:T(8,128)}, f32[128,2048]{1,0:T(8,128)S(1)}) fusion(f32[3,128,2048]{2,1,0:T(8,128)S(1)} %get-tuple-element.95, f32[128,2048]{1,0:T(8,128)S(1)} %get-tuple-element.67, f32[128,2048]{1,0:T(8,128)S(1)} %get-tuple-element.54, f32[2048]{0:T(1024)S(1)} %broadcast_multiply_fusion.2, ...), kind=kLoop, calls=%fused_computation.57 | loop fusion | flops 2359296 | bytes 9445376 | tf_op jit(solution)/shard_map/while/body/eval_jaxpr/transpose(jvp())/broadcast_in_dim | solution.py:31
  82.6 2.2 %multiply_bitcast_fusion.3 = (f32[1,128,2048]{2,1,0:T(8,128)S(1)}, f32[128,2048]{1,0:T(8,128)}, f32[1,128,2048]{2,1,0:T(8,128)S(1)}, f32[128,2048]{1,0:T(8,128)}...) fusion(f32[3,128,2048]{2,1,0:T(8,128)S(1)} %get-tuple-element.95, f32[128,2048]{1,0:T(8,128)S(1)} %get-tuple-element.66, ...), kind=kLoop, calls=%fused_computation.55 | loop fusion | flops 5236736 | bytes 11575296 | tf_op jit(solution)/shard_map/while/body/eval_jaxpr/transpose(jvp())/broadcast_in_dim | solution.py:30
  84.9 4.8 %multiply_bitcast_fusion.11 = (f32[1,128,2048]{2,1,0:T(8,128)S(1)}, f32[1,128,2048]{2,1,0:T(8,128)S(1)}, f32[1,128,2048]{2,1,0:T(8,128)S(1)}, f32[1,128,2048]{2,...) fusion(f32[128,2048]{1,0:T(8,128)} %get-tuple-element.56, ...), kind=kLoop, calls=%fused_computation.65 | loop fusion | flops 3145728 | bytes 18874368 | tf_op jit(solution)/shard_map/while/body/eval_jaxpr/transpose(jvp())/broadcast_in_dim | solution.py:31
  89.7 3.4 %fusion.27 = (f32[3,128]{1,0:T(4,128)S(1)}, f32[3,2048]{1,0:T(4,128)S(1)}) fusion(f32[1,128,2048]{2,1,0:T(8,128)} %get-tuple-element.88, f32[1,128,2048]{2,1,0:T(8,128)S(1)} %get-tuple-element.70, f32[1,128,2048]{2,1,0:T(8,128)} %get-tuple-element.89, f32[1,128,2048]{2,1,0:T(8,128)S(1)} %get-tuple-element.58, f32[1,128,2048]{2,1,0:T(8,128)} %get-tuple-element.90, ...), kind=kLoop, calls=%fused_computation.111 | loop fusion | flops 11003520 | bytes 9490944 | tf_op jit(solution)/shard_map/while/body/eval_jaxpr/transpose(jvp())/reduce_sum | solution.py:26
  93.1 0.0 copy-done
  93.1 0.0 copy-start.1
  93.1 1.9 %fusion.26 = (f32[3,128]{1,0:T(4,128)S(1)}, f32[3,2048]{1,0:T(4,128)S(1)}) fusion(f32[1,128,2048]{2,1,0:T(8,128)S(1)} %get-tuple-element.84, f32[1,128,2048]{2,1,0:T(8,128)S(1)} %get-tuple-element.85, f32[1,128,2048]{2,1,0:T(8,128)S(1)} %get-tuple-element.86, f32[1,128,2048]{2,1,0:T(8,128)S(1)} %copy-done, f32[1,128,2048]{2,1,0:T(8,128)S(1)} %get-tuple-element.73, ...), kind=kLoop, calls=%fused_computation.110 | loop fusion | flops 11789952 | bytes 9490944 | tf_op jit(solution)/shard_map/while/body/eval_jaxpr/transpose(jvp())/reduce_sum | solution.py:27
  95.0 0.1 copy.31
  95.1 0.1 copy.30
  95.2 1.0 scatter_custom_fusion
  96.2 1.2 scatter_fusion
  97.5 0.0 copy-done.1
  97.5 0.1 add_multiply_fusion.1
  97.6 0.6 pad_maximum_fusion
  98.2 0.0 reduce-scatter.2.cloned.1.call-update
  98.3 2.2 %collective-permute-start.1 = (f32[3,1]{0,1:T(1,128)S(1)}, f32[3,1]{0,1:T(1,128)S(1)}, u32[]{:S(2)}, u32[]{:S(2)}) collective-permute-start(f32[3,1]{0,1:T(1,128)S(1)} %slice.108), channel_id=1, source_target_pairs={{0,1},{1,2},{2,3},{3,4},{4,5},{5,6},{6,7},{7,8},{8,9},{9,10},{10,1... | collective-permute-start | bytes 44 | tf_op jit(solution)/shard_map/ppermute | solution.py:14
  100.5 0.1 copy.33
  100.6 0.7 collective-permute-done.1
  101.3 0.1 copy.32
  101.4 0.7 maximum_multiply_fusion
  102.1 45.5 %reduce-scatter.2.cloned.1.call-done = f32[6,128]{1,0:T(8,128)} async-done(((f32[6,2048]{1,0:T(8,128)}), f32[6,128]{1,0:T(8,128)}) %reduce-scatter.2.cloned.1.call-update) | async-done | bytes 3088 | tf_op jit(solution)/shard_map/reduce_scatter | solution.py:94
  (17 shorter events, 0.2 us)
Async XLA Ops:
  7.2 140.4 %reduce-scatter.2.cloned.1.call-start = ((), (), s32[]{:S(2)}) async-start(), calls=%async_computation.1 | async-start | bytes 69632 | tf_op jit(solution)/shard_map/reduce_scatter | solution.py:94
  7.2 64.1 %collective-permute-start = (f32[3,1]{1,0:T(4,128)}, f32[3,1]{1,0:T(4,128)S(1)}, u32[]{:S(2)}, u32[]{:S(2)}) collective-permute-start(f32[3,1]{1,0:T(4,128)} %bitcast.141), channel_id=1, source_target_pairs={{1,0},{2,1},{3,2},{4,3},{5,4},{6,5},{7,6},{8,7},{9,8},{10,9},{11,1... | collective-permute-start | bytes 44 | tf_op jit(solution)/shard_map/ppermute | solution.py:14
  74.5 0.7 copy-start.2
  74.5 0.7 copy-start.3
  89.7 3.4 %copy-start = (f32[1,128,2048]{2,1,0:T(8,128)S(1)}, f32[1,128,2048]{2,1,0:T(8,128)}, u32[]{:S(2)}) copy-start(f32[1,128,2048]{2,1,0:T(8,128)} %get-tuple-element.87) | copy-start | bytes 3145732
  93.1 4.4 %copy-start.1 = (f32[3]{0:T(128)S(1)}, f32[3]{0:T(128)}, u32[]{:S(2)}) copy-start(f32[3]{0:T(128)} %constant.34.clone) | copy-start | bytes 40
  98.3 3.1 %collective-permute-start.1 = (f32[3,1]{0,1:T(1,128)S(1)}, f32[3,1]{0,1:T(1,128)S(1)}, u32[]{:S(2)}, u32[]{:S(2)}) collective-permute-start(f32[3,1]{0,1:T(1,128)S(1)} %slice.108), channel_id=1, source_target_pairs={{0,1},{1,2},{2,3},{3,4},{4,5},{5,6},{6,7},{7,8},{8,9},{9,10},{10,1... | collective-permute-start | bytes 44 | tf_op jit(solution)/shard_map/ppermute | solution.py:14
Sparse Core Ops, SparseCore 0:
  98.4 49.1 reduce-scatter.1
where the time goes:
time: 155 us; the launch traced here: 154 us
  blocking collectives  60.7 us (39%)
  waiting for transfers between devices  46.3 us (30%)
  other arithmetic  25.1 us (16%)
  between operations  14.3 us (9%)
  starting transfers between devices  3.57 us (2%)
  local copies, waits for them, and re-layouts  2.68 us (2%)
  matrix products  1.85 us (1%)
    reduce_scatter x1, waiting for transfers between devices, on_device(): lax.psum_scatter(receiver_buffer, 'src', scatter_dimension=1, tiled=True)  45.5 us
    all_gather x1, blocking collectives, on_device(): shard_points = lax.all_gather(points, 'src', axis=1, tiled=True)  23.8 us
    all_gather x1, blocking collectives, on_device(): shard_left = lax.all_gather(left_modes, 'src', axis=1, tiled=True)  19.2 us
    all_gather x1, blocking collectives, on_device(): shard_normals = lax.all_gather(rcv_normals, 'src', axis=1, tiled=True)  17.7 us
    broadcast_in_dim x2, other arithmetic, tile_energy(): cross_z = rel_first[0] * rel_second[1] - rel_first[1] * rel_second[0]  6.79 us
    ppermute x2, starting transfers between devices, shifted(): lax.ppermute(value, axis, [(source, source + steps) for source in range(l...  3.54 us
    reduce_sum x1, other arithmetic, tile_energy(): rel_first = points[:, None, :] - first_end[:, :, None]  3.41 us
  transfers between devices with their start and end apart: 3, of which 2 were waited for; matrix products, arithmetic and copies ran while one was open for 2% of the time, Pallas kernels for 0%

commit v1 on v0

--- a/solution.py
+++ b/solution.py
@@ -6,6 +6,19 @@
 
 core_term = 0.05
 inverse_four_pi = 0.25 / math.pi
+
+
+def gather_around(value, axis, dim):
+    ways = lax.axis_size(axis)
+    up = [(d, (d + 1) % ways) for d in range(ways)]
+    down = [(d, (d - 1) % ways) for d in range(ways)]
+    earlier, later = ([value], [value])
+    for _ in range(ways // 2):
+        earlier.append(lax.ppermute(earlier[-1], axis, up))
+    for _ in range((ways - 1) // 2):
+        later.append(lax.ppermute(later[-1], axis, down))
+    line = jnp.concatenate([*earlier[::-1], *later[1:]], axis=dim)
+    return jnp.roll(line, (lax.axis_index(axis) - ways // 2) * value.shape[dim], axis=dim)
 
 
 def shifted(value, axis, steps):
@@ -72,7 +85,7 @@
     )
     shard_points = lax.all_gather(points, "src", axis=1, tiled=True)
     shard_normals = lax.all_gather(rcv_normals, "src", axis=1, tiled=True)
-    shard_left = lax.all_gather(left_modes, "src", axis=1, tiled=True)
+    shard_left = gather_around(left_modes, "src", 1)
     row_count = shard_points.shape[1]
     width_rows = math.gcd(row_count, 2048)
 

time: 155 us -> 180 us (1.16)
  starting transfers between devices: 3.57 us -> 35 us
  blocking collectives: 60.7 us -> 37.8 us
  waiting for transfers between devices: 46.3 us -> 62.7 us
    ppermute x0 -> x15, starting transfers between devices: none -> 32.4 us  [the longest x7 31.5 us: gather_around(): later.append(lax.ppermute(later[-1], axis, down))]
    all_gather x1 -> x0, blocking collectives: 19.2 us -> none  [on_device(): shard_left = lax.all_gather(left_modes, 'src', axis=1, tiled=True)]
    ppermute x0 -> x15, waiting for transfers between devices: none -> 11.6 us  [the longest x7 6.21 us: gather_around(): later.append(lax.ppermute(later[-1], axis, down))]
    reduce_scatter x1, waiting for transfers between devices: 45.5 us -> 50.4 us  [on_device(): lax.psum_scatter(receiver_buffer, 'src', scatter_dimension=1, tiled=True)]
    all_gather x1, blocking collectives: 23.8 us -> 20 us  [on_device(): shard_points = lax.all_gather(points, 'src', axis=1, tiled=True)]
  transfers between devices with their start and end apart: 3 -> 18, of which waited for: 2 -> 9; matrix products, arithmetic and copies ran while one was open for 2% -> 4% of each run, Pallas kernels for 0% -> 0%
where the time goes in v1:
time: 180 us
  waiting for transfers between devices  62.7 us (35%)
  blocking collectives  37.8 us (21%)
  starting transfers between devices  35 us (19%)
  other arithmetic  25 us (14%)
  between operations  14.5 us (8%)
  local copies, waits for them, and re-layouts  2.77 us (2%)
  matrix products  1.87 us (1%)
    reduce_scatter x1, waiting for transfers between devices, on_device(): lax.psum_scatter(receiver_buffer, 'src', scatter_dimension=1, tiled=True)  50.4 us
    ppermute x7, starting transfers between devices, gather_around(): later.append(lax.ppermute(later[-1], axis, down))  31.5 us
    all_gather x1, blocking collectives, on_device(): shard_points = lax.all_gather(points, 'src', axis=1, tiled=True)  20 us
    all_gather x1, blocking collectives, on_device(): shard_normals = lax.all_gather(rcv_normals, 'src', axis=1, tiled=True)  17.7 us
    broadcast_in_dim x2, other arithmetic, tile_energy(): cross_z = rel_first[0] * rel_second[1] - rel_first[1] * rel_second[0]  6.8 us
    ppermute x7, waiting for transfers between devices, gather_around(): later.append(lax.ppermute(later[-1], axis, down))  6.21 us
    ppermute x8, waiting for transfers between devices, gather_around(): earlier.append(lax.ppermute(earlier[-1], axis, up))  5.41 us
  transfers between devices with their start and end apart: 18, of which 9 were waited for; matrix products, arithmetic and copies ran while one was open for 4% of the time, Pallas kernels for 0%

profile of v1, /device:TPU:0, one launch (start us, length us, event | category | flops | bytes accessed | tf_op | source)
XLA Modules:
  0.0 179.7 jit_solution(8626271008787293637)
XLA Ops:
  7.2 0.5 collective-permute-start.1
  7.7 5.1 %collective-permute-start.9 = (f32[8,128]{1,0:T(8,128)}, f32[8,128]{1,0:T(8,128)S(1)}, u32[]{:S(2)}, u32[]{:S(2)}) collective-permute-start(f32[8,128]{1,0:T(8,128)} %param.10), channel_id=1, source_target_pairs={{0,15},{1,0},{2,1},{3,2},{4,3},{5,4},{6,5},{7,6},{8,7},{9,8},{10,9... | collective-permute-start | bytes 12296 | tf_op jit(solution)/shard_map/ppermute | solution.py:19
  12.8 1.3 collective-permute-start
  14.1 0.7 multiply_add_fusion.1
  14.8 0.7 slice.81
  15.5 20.0 %all_gather.7 = f32[3,2048]{1,0:T(4,128)S(1)} all-gather(f32[3,128]{1,0:T(4,128)S(1)} %pad_maximum_fusion.3), channel_id=1, replica_groups=mesh['group'=2,'src'=16] {'src'}, dimensions={1}, use_global_device_ids=true | all-gather | bytes 26112 | tf_op jit(solution)/shard_map/all_gather | solution.py:86
  35.5 17.7 %all_gather.6 = f32[3,2048]{1,0:T(4,128)S(1)} all-gather(f32[3,128]{1,0:T(4,128)} %param.9), channel_id=1, replica_groups=mesh['group'=2,'src'=16] {'src'}, dimensions={1}, use_global_device_ids=true | all-gather | bytes 26112 | tf_op jit(solution)/shard_map/all_gather | solution.py:87
  53.3 0.7 fusion.25
  54.0 0.8 pad_maximum_fusion.1
  54.7 0.3 collective-permute-start.2
  55.1 5.4 %collective-permute-done.2 = f32[8,128]{1,0:T(8,128)S(1)} collective-permute-done((f32[8,128]{1,0:T(8,128)S(1)}, f32[8,128]{1,0:T(8,128)S(1)}, u32[]{:S(2)}, u32[]{:S(2)}) %collective-permute-start.2) | collective-permute-done | bytes 4128 | tf_op jit(solution)/shard_map/ppermute | solution.py:17
  60.5 0.1 copy.26
  60.6 0.6 gather_fusion.1
  61.3 0.7 gather_fusion
  62.0 4.5 %collective-permute-start.10 = (f32[8,128]{1,0:T(8,128)S(1)}, f32[8,128]{1,0:T(8,128)S(1)}, u32[]{:S(2)}, u32[]{:S(2)}) collective-permute-start(f32[8,128]{1,0:T(8,128)S(1)} %collective-permute-done.9), channel_id=1, source_target_pairs={{0,15},{1,0},{2,1},{3,2},{4,3},{5,4},{6,5},{7,6},{8,7},{9,8},{10,9... | collective-permute-start | bytes 12296 | tf_op jit(solution)/shard_map/ppermute | solution.py:19
  66.5 0.8 fusion.15
  67.3 0.5 collective-permute-done.10
  67.8 4.4 %collective-permute-start.11 = (f32[8,128]{1,0:T(8,128)S(1)}, f32[8,128]{1,0:T(8,128)S(1)}, u32[]{:S(2)}, u32[]{:S(2)}) collective-permute-start(f32[8,128]{1,0:T(8,128)S(1)} %collective-permute-done.10), channel_id=1, source_target_pairs={{0,15},{1,0},{2,1},{3,2},{4,3},{5,4},{6,5},{7,6},{8,7},{9,8},{10,9... | collective-permute-start | bytes 12296 | tf_op jit(solution)/shard_map/ppermute | solution.py:19
  72.3 0.3 multiply_divide_fusion.1
  72.6 0.9 collective-permute-done.11
  73.6 4.4 %collective-permute-start.12 = (f32[8,128]{1,0:T(8,128)S(1)}, f32[8,128]{1,0:T(8,128)S(1)}, u32[]{:S(2)}, u32[]{:S(2)}) collective-permute-start(f32[8,128]{1,0:T(8,128)S(1)} %collective-permute-done.11), channel_id=1, source_target_pairs={{0,15},{1,0},{2,1},{3,2},{4,3},{5,4},{6,5},{7,6},{8,7},{9,8},{10,9... | collective-permute-start | bytes 12296 | tf_op jit(solution)/shard_map/ppermute | solution.py:19
  78.0 0.3 multiply_divide_fusion.2
  78.3 1.0 collective-permute-done.12
  79.3 4.4 %collective-permute-start.13 = (f32[8,128]{1,0:T(8,128)S(1)}, f32[8,128]{1,0:T(8,128)S(1)}, u32[]{:S(2)}, u32[]{:S(2)}) collective-permute-start(f32[8,128]{1,0:T(8,128)S(1)} %collective-permute-done.12), channel_id=1, source_target_pairs={{0,15},{1,0},{2,1},{3,2},{4,3},{5,4},{6,5},{7,6},{8,7},{9,8},{10,9... | collective-permute-start | bytes 12296 | tf_op jit(solution)/shard_map/ppermute | solution.py:19
  83.7 1.3 collective-permute-done.13
  85.0 4.4 %collective-permute-start.14 = (f32[8,128]{1,0:T(8,128)S(1)}, f32[8,128]{1,0:T(8,128)S(1)}, u32[]{:S(2)}, u32[]{:S(2)}) collective-permute-start(f32[8,128]{1,0:T(8,128)S(1)} %collective-permute-done.13), channel_id=1, source_target_pairs={{0,15},{1,0},{2,1},{3,2},{4,3},{5,4},{6,5},{7,6},{8,7},{9,8},{10,9... | collective-permute-start | bytes 12296 | tf_op jit(solution)/shard_map/ppermute | solution.py:19
  89.4 1.3 collective-permute-done.14
  90.7 4.4 %collective-permute-start.15 = (f32[8,128]{1,0:T(8,128)S(1)}, f32[8,128]{1,0:T(8,128)S(1)}, u32[]{:S(2)}, u32[]{:S(2)}) collective-permute-start(f32[8,128]{1,0:T(8,128)S(1)} %collective-permute-done.14), channel_id=1, source_target_pairs={{0,15},{1,0},{2,1},{3,2},{4,3},{5,4},{6,5},{7,6},{8,7},{9,8},{10,9... | collective-permute-start | bytes 12296 | tf_op jit(solution)/shard_map/ppermute | solution.py:19
  95.3 1.2 collective-permute-done.15
  96.6 1.9 %divide_multiply_fusion.1 = (f32[128,2048]{1,0:T(8,128)S(1)}, f32[128,2048]{1,0:T(8,128)S(1)}, f32[128,2048]{1,0:T(8,128)S(1)}, f32[128,2048]{1,0:T(8,128)S(1)},...) fusion(f32[128]{0:T(128)S(1)} %add_multiply_fusion.2, f32[2048]{0:T(1024)S(1)} %bitcast.135, ...), kind=kOutput, calls=%fused_computation.143 | convolution fusion | flops 31196160 | bytes 13726724 | tf_op jit(solution)/shard_map/while/body/eval_jaxpr/mj,mi->ji/dot_general | solution.py:98
  98.5 2.5 %multiply_reduce_fusion = (f32[3,128]{1,0:T(4,128)S(1)}, f32[128,2048]{1,0:T(8,128)S(1)}, f32[128,2048]{1,0:T(8,128)S(1)}, f32[128,2048]{1,0:T(8,128)S(1)}) fusion(f32[128,2048]{1,0:T(8,128)S(1)} %get-tuple-element.62, f32[128,2048]{1,0:T(8,128)S(1)} %get-tuple-element.92, f32[3,128]{1,0:T(4,128)S(1)} %bitcast.126, f32[128,2048]{1,0:T(8,128)S(1)} %get-tuple-element.94, ...), kind=kLoop, calls=%fused_computation.36 | loop fusion | flops 12582528 | bytes 8419328 | tf_op jit(solution)/shard_map/while/body/eval_jaxpr/transpose(jvp())/reduce_sum | solution.py:48
  101.0 0.2 multiply_multiply_fusion.3
  101.2 0.2 multiply_multiply_fusion.1
  101.4 0.5 fusion.30
  101.9 2.0 %multiply_bitcast_fusion.5 = (f32[1,128,2048]{2,1,0:T(8,128)}, f32[128,2048]{1,0:T(8,128)}, f32[128,2048]{1,0:T(8,128)S(1)}) fusion(f32[3,128,2048]{2,1,0:T(8,128)S(1)} %get-tuple-element.95, f32[128,2048]{1,0:T(8,128)S(1)} %get-tuple-element.67, f32[128,2048]{1,0:T(8,128)S(1)} %get-tuple-element.54, f32[2048]{0:T(1024)S(1)} %broadcast_multiply_fusion.2, ...), kind=kLoop, calls=%fused_computation.57 | loop fusion | flops 2359296 | bytes 9445376 | tf_op jit(solution)/shard_map/while/body/eval_jaxpr/transpose(jvp())/broadcast_in_dim | solution.py:44
  103.9 2.3 %multiply_bitcast_fusion.3 = (f32[1,128,2048]{2,1,0:T(8,128)S(1)}, f32[128,2048]{1,0:T(8,128)}, f32[1,128,2048]{2,1,0:T(8,128)S(1)}, f32[128,2048]{1,0:T(8,128)}...) fusion(f32[3,128,2048]{2,1,0:T(8,128)S(1)} %get-tuple-element.95, f32[128,2048]{1,0:T(8,128)S(1)} %get-tuple-element.66, ...), kind=kLoop, calls=%fused_computation.55 | loop fusion | flops 5236736 | bytes 11575296 | tf_op jit(solution)/shard_map/while/body/eval_jaxpr/transpose(jvp())/broadcast_in_dim | solution.py:43
  106.2 4.8 %multiply_bitcast_fusion.11 = (f32[1,128,2048]{2,1,0:T(8,128)S(1)}, f32[1,128,2048]{2,1,0:T(8,128)S(1)}, f32[1,128,2048]{2,1,0:T(8,128)S(1)}, f32[1,128,2048]{2,...) fusion(f32[128,2048]{1,0:T(8,128)} %get-tuple-element.56, ...), kind=kLoop, calls=%fused_computation.65 | loop fusion | flops 3145728 | bytes 18874368 | tf_op jit(solution)/shard_map/while/body/eval_jaxpr/transpose(jvp())/broadcast_in_dim | solution.py:44
  111.0 3.4 %fusion.29 = (f32[3,128]{1,0:T(4,128)S(1)}, f32[3,2048]{1,0:T(4,128)S(1)}) fusion(f32[1,128,2048]{2,1,0:T(8,128)} %get-tuple-element.88, f32[1,128,2048]{2,1,0:T(8,128)S(1)} %get-tuple-element.70, f32[1,128,2048]{2,1,0:T(8,128)} %get-tuple-element.89, f32[1,128,2048]{2,1,0:T(8,128)S(1)} %get-tuple-element.58, f32[1,128,2048]{2,1,0:T(8,128)} %get-tuple-element.90, ...), kind=kLoop, calls=%fused_computation.145 | loop fusion | flops 11003520 | bytes 9490944 | tf_op jit(solution)/shard_map/while/body/eval_jaxpr/transpose(jvp())/reduce_sum | solution.py:39
  114.4 1.9 %fusion.28 = (f32[3,128]{1,0:T(4,128)S(1)}, f32[3,2048]{1,0:T(4,128)S(1)}) fusion(f32[1,128,2048]{2,1,0:T(8,128)S(1)} %get-tuple-element.84, f32[1,128,2048]{2,1,0:T(8,128)S(1)} %get-tuple-element.85, f32[1,128,2048]{2,1,0:T(8,128)S(1)} %get-tuple-element.86, f32[1,128,2048]{2,1,0:T(8,128)S(1)} %copy-done, f32[1,128,2048]{2,1,0:T(8,128)S(1)} %get-tuple-element.73, ...), kind=kLoop, calls=%fused_computation.144 | loop fusion | flops 11789952 | bytes 9490944 | tf_op jit(solution)/shard_map/while/body/eval_jaxpr/transpose(jvp())/reduce_sum | solution.py:40
  116.3 0.1 copy.31
  116.4 0.1 copy.30
  116.5 1.0 scatter_custom_fusion
  117.5 1.2 scatter_fusion
  118.9 0.6 pad_maximum_fusion
  119.6 1.3 collective-permute-start.16
  121.0 0.7 collective-permute-done.16
  121.8 0.7 maximum_multiply_fusion
  122.4 50.4 %reduce-scatter.2.cloned.1.call-done = f32[6,128]{1,0:T(8,128)} async-done(((f32[6,2048]{1,0:T(8,128)}), f32[6,128]{1,0:T(8,128)}) %reduce-scatter.2.cloned.1.call-update) | async-done | bytes 3088 | tf_op jit(solution)/shard_map/reduce_scatter | solution.py:107
  (80 shorter events, 0.7 us)
Async XLA Ops:
  7.2 165.7 %reduce-scatter.2.cloned.1.call-start = ((), (), s32[]{:S(2)}) async-start(), calls=%async_computation.1 | async-start | bytes 69632 | tf_op jit(solution)/shard_map/reduce_scatter | solution.py:107
  7.2 47.5 %collective-permute-start.1 = (f32[8,128]{1,0:T(8,128)}, f32[8,128]{1,0:T(8,128)S(1)}, u32[]{:S(2)}, u32[]{:S(2)}) collective-permute-start(f32[8,128]{1,0:T(8,128)} %param.10), channel_id=1, source_target_pairs={{0,1},{1,2},{2,3},{3,4},{4,5},{5,6},{6,7},{7,8},{8,9},{9,10},{10,1... | collective-permute-start | bytes 12296 | tf_op jit(solution)/shard_map/ppermute | solution.py:17
  7.7 54.3 %collective-permute-start.9 = (f32[8,128]{1,0:T(8,128)}, f32[8,128]{1,0:T(8,128)S(1)}, u32[]{:S(2)}, u32[]{:S(2)}) collective-permute-start(f32[8,128]{1,0:T(8,128)} %param.10), channel_id=1, source_target_pairs={{0,15},{1,0},{2,1},{3,2},{4,3},{5,4},{6,5},{7,6},{8,7},{9,8},{10,9... | collective-permute-start | bytes 12296 | tf_op jit(solution)/shard_map/ppermute | solution.py:19
  12.8 41.2 %collective-permute-start = (f32[3,1]{1,0:T(4,128)}, f32[3,1]{1,0:T(4,128)S(1)}, u32[]{:S(2)}, u32[]{:S(2)}) collective-permute-start(f32[3,1]{1,0:T(4,128)} %bitcast.140), channel_id=1, source_target_pairs={{1,0},{2,1},{3,2},{4,3},{5,4},{6,5},{7,6},{8,7},{9,8},{10,9},{11,1... | collective-permute-start | bytes 44 | tf_op jit(solution)/shard_map/ppermute | solution.py:27
  54.7 5.7 %collective-permute-start.2 = (f32[8,128]{1,0:T(8,128)S(1)}, f32[8,128]{1,0:T(8,128)S(1)}, u32[]{:S(2)}, u32[]{:S(2)}) collective-permute-start(f32[8,128]{1,0:T(8,128)S(1)} %collective-permute-done.1), channel_id=1, source_target_pairs={{0,1},{1,2},{2,3},{3,4},{4,5},{5,6},{6,7},{7,8},{8,9},{9,10},{10,1... | collective-permute-start | bytes 12296 | tf_op jit(solution)/shard_map/ppermute | solution.py:17
  60.5 6.0 %collective-permute-start.3 = (f32[8,128]{1,0:T(8,128)S(1)}, f32[8,128]{1,0:T(8,128)S(1)}, u32[]{:S(2)}, u32[]{:S(2)}) collective-permute-start(f32[8,128]{1,0:T(8,128)S(1)} %collective-permute-done.2), channel_id=1, source_target_pairs={{0,1},{1,2},{2,3},{3,4},{4,5},{5,6},{6,7},{7,8},{8,9},{9,10},{10,1... | collective-permute-start | bytes 12296 | tf_op jit(solution)/shard_map/ppermute | solution.py:17
  62.0 5.8 %collective-permute-start.10 = (f32[8,128]{1,0:T(8,128)S(1)}, f32[8,128]{1,0:T(8,128)S(1)}, u32[]{:S(2)}, u32[]{:S(2)}) collective-permute-start(f32[8,128]{1,0:T(8,128)S(1)} %collective-permute-done.9), channel_id=1, source_target_pairs={{0,15},{1,0},{2,1},{3,2},{4,3},{5,4},{6,5},{7,6},{8,7},{9,8},{10,9... | collective-permute-start | bytes 12296 | tf_op jit(solution)/shard_map/ppermute | solution.py:19
  66.5 5.7 %collective-permute-start.4 = (f32[8,128]{1,0:T(8,128)S(1)}, f32[8,128]{1,0:T(8,128)S(1)}, u32[]{:S(2)}, u32[]{:S(2)}) collective-permute-start(f32[8,128]{1,0:T(8,128)S(1)} %collective-permute-done.3), channel_id=1, source_target_pairs={{0,1},{1,2},{2,3},{3,4},{4,5},{5,6},{6,7},{7,8},{8,9},{9,10},{10,1... | collective-permute-start | bytes 12296 | tf_op jit(solution)/shard_map/ppermute | solution.py:17
  67.8 5.7 %collective-permute-start.11 = (f32[8,128]{1,0:T(8,128)S(1)}, f32[8,128]{1,0:T(8,128)S(1)}, u32[]{:S(2)}, u32[]{:S(2)}) collective-permute-start(f32[8,128]{1,0:T(8,128)S(1)} %collective-permute-done.10), channel_id=1, source_target_pairs={{0,15},{1,0},{2,1},{3,2},{4,3},{5,4},{6,5},{7,6},{8,7},{9,8},{10,9... | collective-permute-start | bytes 12296 | tf_op jit(solution)/shard_map/ppermute | solution.py:19
  72.2 5.7 %collective-permute-start.5 = (f32[8,128]{1,0:T(8,128)S(1)}, f32[8,128]{1,0:T(8,128)S(1)}, u32[]{:S(2)}, u32[]{:S(2)}) collective-permute-start(f32[8,128]{1,0:T(8,128)S(1)} %collective-permute-done.4), channel_id=1, source_target_pairs={{0,1},{1,2},{2,3},{3,4},{4,5},{5,6},{6,7},{7,8},{8,9},{9,10},{10,1... | collective-permute-start | bytes 12296 | tf_op jit(solution)/shard_map/ppermute | solution.py:17
  72.2 23.0 %copy-start.1 = (f32[8,128]{1,0:T(8,128)S(1)}, f32[8,128]{1,0:T(8,128)}, u32[]{:S(2)}) copy-start(f32[8,128]{1,0:T(8,128)} %param.10) | copy-start | bytes 12292
  72.2 24.4 %copy-start.3 = (f32[8,128]{1,0:T(8,128)S(1)}, f32[8,128]{1,0:T(8,128)}, u32[]{:S(2)}) copy-start(f32[8,128]{1,0:T(8,128)} %param.13) | copy-start | bytes 12292
  72.3 24.4 %copy-start.4 = (f32[8]{0:T(128)S(1)}, f32[8]{0:T(128)}, u32[]{:S(2)}) copy-start(f32[8]{0:T(128)} %param.14) | copy-start | bytes 100
  73.6 5.7 %collective-permute-start.12 = (f32[8,128]{1,0:T(8,128)S(1)}, f32[8,128]{1,0:T(8,128)S(1)}, u32[]{:S(2)}, u32[]{:S(2)}) collective-permute-start(f32[8,128]{1,0:T(8,128)S(1)} %collective-permute-done.11), channel_id=1, source_target_pairs={{0,15},{1,0},{2,1},{3,2},{4,3},{5,4},{6,5},{7,6},{8,7},{9,8},{10,9... | collective-permute-start | bytes 12296 | tf_op jit(solution)/shard_map/ppermute | solution.py:19
  78.0 5.7 %collective-permute-start.6 = (f32[8,128]{1,0:T(8,128)S(1)}, f32[8,128]{1,0:T(8,128)S(1)}, u32[]{:S(2)}, u32[]{:S(2)}) collective-permute-start(f32[8,128]{1,0:T(8,128)S(1)} %collective-permute-done.5), channel_id=1, source_target_pairs={{0,1},{1,2},{2,3},{3,4},{4,5},{5,6},{6,7},{7,8},{8,9},{9,10},{10,1... | collective-permute-start | bytes 12296 | tf_op jit(solution)/shard_map/ppermute | solution.py:17
  79.3 5.7 %collective-permute-start.13 = (f32[8,128]{1,0:T(8,128)S(1)}, f32[8,128]{1,0:T(8,128)S(1)}, u32[]{:S(2)}, u32[]{:S(2)}) collective-permute-start(f32[8,128]{1,0:T(8,128)S(1)} %collective-permute-done.12), channel_id=1, source_target_pairs={{0,15},{1,0},{2,1},{3,2},{4,3},{5,4},{6,5},{7,6},{8,7},{9,8},{10,9... | collective-permute-start | bytes 12296 | tf_op jit(solution)/shard_map/ppermute | solution.py:19
  83.7 5.7 %collective-permute-start.7 = (f32[8,128]{1,0:T(8,128)S(1)}, f32[8,128]{1,0:T(8,128)S(1)}, u32[]{:S(2)}, u32[]{:S(2)}) collective-permute-start(f32[8,128]{1,0:T(8,128)S(1)} %collective-permute-done.6), channel_id=1, source_target_pairs={{0,1},{1,2},{2,3},{3,4},{4,5},{5,6},{6,7},{7,8},{8,9},{9,10},{10,1... | collective-permute-start | bytes 12296 | tf_op jit(solution)/shard_map/ppermute | solution.py:17
  85.0 5.7 %collective-permute-start.14 = (f32[8,128]{1,0:T(8,128)S(1)}, f32[8,128]{1,0:T(8,128)S(1)}, u32[]{:S(2)}, u32[]{:S(2)}) collective-permute-start(f32[8,128]{1,0:T(8,128)S(1)} %collective-permute-done.13), channel_id=1, source_target_pairs={{0,15},{1,0},{2,1},{3,2},{4,3},{5,4},{6,5},{7,6},{8,7},{9,8},{10,9... | collective-permute-start | bytes 12296 | tf_op jit(solution)/shard_map/ppermute | solution.py:19
  89.4 5.7 %collective-permute-start.8 = (f32[8,128]{1,0:T(8,128)S(1)}, f32[8,128]{1,0:T(8,128)S(1)}, u32[]{:S(2)}, u32[]{:S(2)}) collective-permute-start(f32[8,128]{1,0:T(8,128)S(1)} %collective-permute-done.7), channel_id=1, source_target_pairs={{0,1},{1,2},{2,3},{3,4},{4,5},{5,6},{6,7},{7,8},{8,9},{9,10},{10,1... | collective-permute-start | bytes 12296 | tf_op jit(solution)/shard_map/ppermute | solution.py:17
  90.7 5.7 %collective-permute-start.15 = (f32[8,128]{1,0:T(8,128)S(1)}, f32[8,128]{1,0:T(8,128)S(1)}, u32[]{:S(2)}, u32[]{:S(2)}) collective-permute-start(f32[8,128]{1,0:T(8,128)S(1)} %collective-permute-done.14), channel_id=1, source_target_pairs={{0,15},{1,0},{2,1},{3,2},{4,3},{5,4},{6,5},{7,6},{8,7},{9,8},{10,9... | collective-permute-start | bytes 12296 | tf_op jit(solution)/shard_map/ppermute | solution.py:19
  111.0 3.4 %copy-start = (f32[1,128,2048]{2,1,0:T(8,128)S(1)}, f32[1,128,2048]{2,1,0:T(8,128)}, u32[]{:S(2)}) copy-start(f32[1,128,2048]{2,1,0:T(8,128)} %get-tuple-element.87) | copy-start | bytes 3145732
  114.4 4.4 %copy-start.2 = (f32[3]{0:T(128)S(1)}, f32[3]{0:T(128)}, u32[]{:S(2)}) copy-start(f32[3]{0:T(128)} %constant.75.clone) | copy-start | bytes 40
  119.6 2.1 %collective-permute-start.16 = (f32[3,1]{0,1:T(1,128)S(1)}, f32[3,1]{0,1:T(1,128)S(1)}, u32[]{:S(2)}, u32[]{:S(2)}) collective-permute-start(f32[3,1]{0,1:T(1,128)S(1)} %slice.108), channel_id=1, source_target_pairs={{0,1},{1,2},{2,3},{3,4},{4,5},{5,6},{6,7},{7,8},{8,9},{9,10},{10,1... | collective-permute-start | bytes 44 | tf_op jit(solution)/shard_map/ppermute | solution.py:27
Sparse Core Ops, SparseCore 0:
  119.7 53.0 reduce-scatter.1
